TPU v7x, 32 devices: a whole 2x2x4 slice. The times are simulated.
32 devices in a mesh: groups: 2 (over y), sect: 16 (over z, x, core).
Axes of the slice: x: 2, y: 2, z: 4, core: 2. Of those that a mesh axis runs over, the one named last changes fastest.
Arguments:
- pattern: int32 [32], P('sect'), may hold values from 0 to 15
- thickness: float32 [32], P('sect'), may hold values from 0.5 to 1.5
- coupling: float32 [16, 2, 169, 169], replicated, may hold values from -0.0625 to 0.0625
- angles: float32 [64, 169], replicated, may hold values from -3.140625 to 3.140625
- points: int32 [2], P('groups'), parts along dimension 0, may hold values from 0 to 63
- incident: float32 [2, 2, 169, 169], P('groups'), parts along dimension 0, may hold values from -6 to 6
- monitors: int32 [16], replicated, may hold values from 0 to 168
- weights: float32 [16], replicated, may hold values from 0.05 to 0.5
Outputs:
- fields: float32 [32, 2, 2, 169, 169], P('sect', 'groups'), parts along dimension 1
- gradient: float32 [2, 32], P('groups', 'sect'), parts along dimension 0
There are 2 independent parts, one for each index of `groups`. A program takes and returns all parts, laid end to end along the dimension named above; an argument that names none is the same for every part. Nothing has to cross between parts.
All inputs are finite; a program needn't handle non-finite values.
Results may differ from a plain program's by a relative error of at most 0.0003.
Values sent between devices are 32-bit elements; how exact they have to be, the bound alone decides.
A program may use at most 128 MiB of HBM per device.

v0:
```python
import jax
import jax.numpy as jnp
from jax import lax
from jax.sharding import PartitionSpec as P

norm_scale = (1.0 + 1.0 / 22.0) ** (-0.5)
highest = lax.Precision.HIGHEST


def entering(shard, axis, combine, identity, reverse):
    length, here = (lax.axis_size(axis), lax.axis_index(axis))
    everything = jax.tree.map(lambda part: lax.all_gather(part, axis), shard)
    start = jax.tree.map(
        lambda part, zero: jnp.broadcast_to(jnp.asarray(zero, part.dtype), part.shape),
        shard,
        identity,
    )

    def hop(k, before):
        at = length - 1 - k if reverse else k
        reached = at > here if reverse else at < here
        new = combine(before, jax.tree.map(lambda part: part[at], everything))
        return jax.tree.map(lambda a, b: jnp.where(reached, a, b), new, before)

    return lax.fori_loop(0, length, hop, start)


def spread(block, axis, source):
    block = jnp.where(lax.axis_index(axis) == source, block, jnp.zeros_like(block))
    return lax.psum(block, axis)


def complex_product(left, right):
    left_real, left_imag = left
    right_real, right_imag = right
    out_real = jnp.einsum("pij,pjk->pik", left_real, right_real, precision=highest) - jnp.einsum(
        "pij,pjk->pik", left_imag, right_imag, precision=highest
    )
    out_imag = jnp.einsum("pij,pjk->pik", left_real, right_imag, precision=highest) + jnp.einsum(
        "pij,pjk->pik", left_imag, right_real, precision=highest
    )
    return (out_real, out_imag)


def combine_forward(earlier, later):
    return complex_product(later, earlier)


def combine_backward(earlier, later):
    return complex_product(earlier, later)


def apply_matrix(matrix, fields_now):
    mat_real, mat_imag = matrix
    vec_real = fields_now[:, 0]
    vec_imag = fields_now[:, 1]
    out_real = jnp.einsum("pij,pjk->pik", mat_real, vec_real, precision=highest) - jnp.einsum(
        "pij,pjk->pik", mat_imag, vec_imag, precision=highest
    )
    out_imag = jnp.einsum("pij,pjk->pik", mat_real, vec_imag, precision=highest) + jnp.einsum(
        "pij,pjk->pik", mat_imag, vec_real, precision=highest
    )
    return jnp.stack([out_real, out_imag], axis=1)


def apply_adjoint(matrix, fields_now):
    mat_real, mat_imag = matrix
    vec_real = fields_now[:, 0]
    vec_imag = fields_now[:, 1]
    out_real = jnp.einsum("pji,pjk->pik", mat_real, vec_real, precision=highest) + jnp.einsum(
        "pji,pjk->pik", mat_imag, vec_imag, precision=highest
    )
    out_imag = jnp.einsum("pji,pjk->pik", mat_real, vec_imag, precision=highest) - jnp.einsum(
        "pji,pjk->pik", mat_imag, vec_real, precision=highest
    )
    return jnp.stack([out_real, out_imag], axis=1)


def local(pattern, thickness, coupling, angles, points, incident, monitors, weights):
    harmonics = incident.shape[2]
    point_count = incident.shape[0]
    local_layers = pattern.shape[0]
    angle_rows = angles[points]
    identity_matrix = jnp.eye(harmonics, dtype=jnp.float32)
    layer_data = []
    for layer_index in range(local_layers):
        mixing_real = norm_scale * (identity_matrix + coupling[pattern[layer_index], 0])
        mixing_imag = norm_scale * coupling[pattern[layer_index], 1]
        phase = angle_rows * thickness[layer_index]
        cosine = jnp.cos(phase)[:, :, None]
        sine_part = jnp.sin(phase)[:, :, None]
        layer_real = cosine * mixing_real[None] - sine_part * mixing_imag[None]
        layer_imag = cosine * mixing_imag[None] + sine_part * mixing_real[None]
        layer_data.append(((layer_real, layer_imag), cosine, sine_part, mixing_real, mixing_imag))
    section = layer_data[0][0]
    layer_index = 1
    section = complex_product(layer_data[layer_index][0], section)
    section_real, section_imag = section
    eye_batch = identity_matrix[None]
    zero_batch = jnp.zeros(section_real.shape, jnp.float32)
    prefix = entering(
        (section_real, section_imag), "sect", combine_forward, (eye_batch, zero_batch), False
    )
    suffix = entering(
        (section_real, section_imag), "sect", combine_backward, (eye_batch, zero_batch), True
    )
    current = apply_matrix(prefix, incident)
    field_list = []
    for layer_index in range(local_layers):
        current = apply_matrix(layer_data[layer_index][0], current)
        field_list.append(current)
    fields = jnp.stack(field_list, axis=0)
    last_field = spread(current, "sect", lax.axis_size("sect") - 1)
    selector = jnp.sum(
        jnp.where(monitors[:, None] == jnp.arange(harmonics)[None, :], weights[:, None], 0.0),
        axis=0,
    )
    adjoint = apply_adjoint(
        suffix, last_field * selector[None, None, :, None] / (point_count * harmonics)
    )
    grad_list = []
    for layer_index in range(local_layers - 1, -1, -1):
        unused_matrix, cosine, sine_part, mixing_real, mixing_imag = layer_data[layer_index]
        layer_field = field_list[layer_index]
        adj_real = adjoint[:, 0]
        adj_imag = adjoint[:, 1]
        grad_list.append(
            -2.0
            * jnp.sum(
                angle_rows[:, :, None]
                * (adj_real * layer_field[:, 1] - adj_imag * layer_field[:, 0])
            )
        )
        back_real = cosine * adj_real + sine_part * adj_imag
        back_imag = cosine * adj_imag - sine_part * adj_real
        new_real = jnp.einsum(
            "ji,pjk->pik", mixing_real, back_real, precision=highest
        ) + jnp.einsum("ji,pjk->pik", mixing_imag, back_imag, precision=highest)
        new_imag = jnp.einsum(
            "ji,pjk->pik", mixing_real, back_imag, precision=highest
        ) - jnp.einsum("ji,pjk->pik", mixing_imag, back_real, precision=highest)
        adjoint = jnp.stack([new_real, new_imag], axis=1)
    gradient = jnp.stack(grad_list[::-1], axis=0)[None, :]
    return (fields, gradient)


def solution(mesh):
    in_specs = (
        P("sect"),
        P("sect"),
        P(),
        P(),
        P("groups"),
        P("groups", None, None, None),
        P(),
        P(),
    )
    out_specs = (P("sect", "groups", None, None, None), P("groups", "sect"))
    return jax.shard_map(local, mesh=mesh, in_specs=in_specs, out_specs=out_specs, check_vma=False)
```

profile of v0, /device:TPU:0, one launch (start us, length us, event | category | flops | bytes accessed | tf_op | source)
XLA Modules:
  0.0 395.3 jit_solution(12122222718518575283)
XLA Ops:
  15.8 1.9 constant_dynamic-slice_fusion.1
  21.6 44.9 %all-gather.9.cloned.1.call-done = f32[16,169,169]{2,1,0:T(8,128)} async-done(((f32[1,169,169]{2,1,0:T(8,128)}), f32[16,169,169]{2,1,0:T(8,128)}) %all-gather.9.cloned.1.call-update) | async-done | bytes 1827920 | tf_op jit(solution)/shard_map/all_gather | solution.py:12
  66.5 45.6 %all-gather.7.cloned.1.call-done = f32[16,169,169]{2,1,0:T(8,128)} async-done(((f32[1,169,169]{2,1,0:T(8,128)}), f32[16,169,169]{2,1,0:T(8,128)}) %all-gather.7.cloned.1.call-update) | async-done | bytes 1827920 | tf_op jit(solution)/shard_map/all_gather | solution.py:12
  112.0 81.1 %while.35 = (s32[]{:T(128)}, f32[1,169,169]{2,1,0:T(8,128)S(1)}, f32[1,169,169]{2,1,0:T(8,128)S(1)}, s32[]{:T(128)}, f32[16,1,169,169]{3,2,1,0:T(8,128)}, /*index=5*/f32[16,1,169,169]{3,2,1,0:T(8,128)}, s32[]{:T(128)}, s32[]{:T(128)}) while((s32[]{:T(128)}, f32[1,169,169]{2,1,0:T(8,128)S(1)}, f32[1,169,169]{2,1,0:T(8,128)S(1)}, ...), condition=%wide.region_1.2_spmd.clone, body=%wide.region_0.1_spmd.clone.sunk | while | flops 231886752 | bytes 2320444 | solution.py:25
  193.1 95.1 %while.36 = (s32[]{:T(128)}, f32[1,169,169]{1,2,0:T(8,128)S(1)}, f32[1,169,169]{1,2,0:T(8,128)S(1)}, s32[]{:T(128)}, f32[16,1,169,169]{3,2,1,0:T(8,128)}, /*inde...) while((s32[]{:T(128)}, f32[1,169,169]{1,2,0:T(8,128)S(1)}, ...), condition=%wide.region_3.4_spmd.clone, body=%wide.region_2.3_spmd.clone.sunk | while | flops 231886752 | bytes 2520487 | solution.py:25
  193.2 1.5 fusion.196
  194.7 1.5 fusion.194
  196.1 1.5 fusion.195
  197.6 1.5 fusion.197
  199.1 1.5 fusion.196
  200.6 1.5 fusion.194
  202.1 1.5 fusion.195
  203.6 1.5 fusion.197
  205.1 1.5 fusion.196
  206.5 1.5 fusion.194
  208.0 1.5 fusion.195
  209.5 1.5 fusion.197
  211.0 1.5 fusion.196
  212.5 1.5 fusion.194
  214.0 1.5 fusion.195
  215.5 1.5 fusion.197
  217.0 1.5 fusion.196
  218.4 1.5 fusion.194
  219.9 1.5 fusion.195
  221.4 1.5 fusion.197
  222.9 1.5 fusion.196
  224.4 1.5 fusion.194
  225.8 1.5 fusion.195
  227.3 1.5 fusion.197
  228.9 1.5 fusion.196
  230.3 1.5 fusion.194
  231.8 1.5 fusion.195
  233.3 1.5 fusion.197
  234.8 1.5 fusion.196
  236.3 1.5 fusion.194
  237.7 1.5 fusion.195
  239.2 1.5 fusion.197
  240.8 1.5 fusion.196
  242.2 1.5 fusion.194
  243.7 1.5 fusion.195
  245.2 1.5 fusion.197
  246.7 1.5 fusion.196
  248.2 1.5 fusion.194
  249.6 1.5 fusion.195
  251.1 1.5 fusion.197
  254.1 1.5 fusion.194
  255.6 1.5 fusion.195
  257.1 1.5 fusion.197
  258.6 1.5 fusion.196
  260.1 1.5 fusion.194
  261.5 1.5 fusion.195
  263.0 1.5 fusion.197
  264.5 1.5 fusion.196
  266.0 1.5 fusion.194
  267.5 1.5 fusion.195
  269.0 1.5 fusion.197
  270.5 1.5 fusion.196
  273.4 1.5 fusion.195
  274.9 1.5 fusion.197
  279.4 1.5 fusion.195
  280.8 1.5 fusion.197
  285.3 1.5 fusion.195
  286.8 1.5 fusion.197
  294.8 86.2 %all-reduce.2.cloned.1.call-done = f32[1,2,169,169]{3,2,1,0:T(8,128)} async-done(((f32[1,2,169,169]{3,2,1,0:T(8,128)}), f32[1,2,169,169]{3,2,1,0:T(8,128)}) %all-reduce.2.cloned.1.call-update) | async-done | bytes 228504 | tf_op jit(solution)/shard_map/psum | solution.py:30
  (156 shorter events, 109.7 us)
Async XLA Ops:
  7.2 6.0 %copy-start = (f32[64,169]{1,0:T(8,128)S(1)}, f32[64,169]{1,0:T(8,128)}, u32[]{:S(2)}) copy-start(f32[64,169]{1,0:T(8,128)} %param.15) | copy-start | bytes 129796
  7.2 59.3 %all-gather.9.cloned.1.call-start = ((), (), s32[]{:S(2)}) async-start(), calls=%async_computation.2 | async-start | bytes 3063808 | tf_op jit(solution)/shard_map/all_gather | solution.py:12
  15.7 5.5 %copy-start.2 = (f32[16]{0:T(128)S(1)}, f32[16]{0:T(128)}, u32[]{:S(2)}) copy-start(f32[16]{0:T(128)} %param.19) | copy-start | bytes 196
  15.8 5.5 %copy-start.3 = (s32[16]{0:T(128)S(1)}, s32[16]{0:T(128)}, u32[]{:S(2)}) copy-start(s32[16]{0:T(128)} %param.18) | copy-start | bytes 196
  15.8 5.5 %copy-start.1 = (f32[1,2,169,169]{3,1,2,0:T(2,128)S(1)}, f32[1,2,169,169]{3,1,2,0:T(2,128)}, u32[]{:S(2)}) copy-start(f32[1,2,169,169]{3,1,2,0:T(2,128)} %param.17) | copy-start | bytes 685468
  19.2 92.8 %all-gather.7.cloned.1.call-start = ((), (), s32[]{:S(2)}) async-start(), calls=%async_computation.1 | async-start | bytes 3063808 | tf_op jit(solution)/shard_map/all_gather | solution.py:12
  20.8 360.1 %all-reduce.2.cloned.1.call-start = ((), (), s32[]{:S(2)}) async-start(), calls=%async_computation | async-start | bytes 720896 | tf_op jit(solution)/shard_map/psum | solution.py:30
Sparse Core Ops, SparseCore 0:
  19.4 47.0 all-gather.8
  69.3 42.6 all-gather.6
  293.4 87.4 all-reduce.1
where the time goes:
time: 399 us; the launch traced here: 395 us
  matrix products  186 us (47%)
  waiting for transfers between devices  177 us (44%)
  between operations  19.9 us (5%)
  local copies, waits for them, and re-layouts  6.83 us (2%)
    all_gather x2, waiting for transfers between devices, entering(): everything = jax.tree.map(lambda part: lax.all_gather(part, axis), shard)  90.4 us
    psum x1, waiting for transfers between devices, spread(): return lax.psum(block, axis)  86.2 us
    dot_general x33, matrix products, complex_product(): jnp.einsum('pij,pjk->pik', left_imag, right_imag, precision=highest)  45.8 us
    dot_general x33, matrix products, complex_product(): jnp.einsum('pij,pjk->pik', left_imag, right_real, precision=highest)  44.1 us
    dot_general x33, matrix products, complex_product(): jnp.einsum('pij,pjk->pik', left_real, right_imag, precision=highest)  43.4 us
    dot_general x33, matrix products, complex_product(): jnp.einsum('pij,pjk->pik', left_real, right_real, precision=highest)  43.4 us
  transfers between devices with their start and end apart: 3, of which 3 were waited for; matrix products, arithmetic and copies ran while one was open for 1% of the time, Pallas kernels for 0%

commit v1 on v0

--- a/solution.py
+++ b/solution.py
@@ -5,6 +5,12 @@
 
 norm_scale = (1.0 + 1.0 / 22.0) ** (-0.5)
 highest = lax.Precision.HIGHEST
+
+
+def summed_here(x, mesh_axis):
+    parts = lax.all_gather(x, mesh_axis, axis=0, tiled=False)
+    total = parts.sum(axis=0)
+    return total
 
 
 def entering(shard, axis, combine, identity, reverse):
@@ -27,7 +33,7 @@
 
 def spread(block, axis, source):
     block = jnp.where(lax.axis_index(axis) == source, block, jnp.zeros_like(block))
-    return lax.psum(block, axis)
+    return summed_here(block, axis)
 
 
 def complex_product(left, right):

time: 399 us -> 317 us (0.79)
  waiting for transfers between devices: 177 us -> 90.7 us
    psum x1 -> x0, waiting for transfers between devices: 86.2 us -> none  [spread(): return lax.psum(block, axis)]
    reduce_sum x0 -> x1, other arithmetic: none -> 4.64 us  [summed_here(): total = parts.sum(axis=0)]
  transfers between devices with their start and end apart: 3 -> 3, of which waited for: 3 -> 2; matrix products, arithmetic and copies ran while one was open for 1% -> 31% of each run, Pallas kernels for 0% -> 0%
where the time goes in v1:
time: 317 us; the launch traced here: 314 us
  matrix products  186 us (59%)
  waiting for transfers between devices  90.7 us (29%)
  between operations  19.9 us (6%)
  local copies, waits for them, and re-layouts  8.09 us (3%)
  other arithmetic  7.04 us (2%)
    all_gather x2, waiting for transfers between devices, entering(): everything = jax.tree.map(lambda part: lax.all_gather(part, axis), shard)  90.6 us
    dot_general x33, matrix products, complex_product(): jnp.einsum('pij,pjk->pik', left_imag, right_imag, precision=highest)  45.8 us
    dot_general x33, matrix products, complex_product(): jnp.einsum('pij,pjk->pik', left_imag, right_real, precision=highest)  44.2 us
    dot_general x33, matrix products, complex_product(): jnp.einsum('pij,pjk->pik', left_real, right_imag, precision=highest)  43.5 us
    dot_general x33, matrix products, complex_product(): jnp.einsum('pij,pjk->pik', left_real, right_real, precision=highest)  43.4 us
  transfers between devices with their start and end apart: 3, of which 2 were waited for; matrix products, arithmetic and copies ran while one was open for 31% of the time, Pallas kernels for 0%

profile of v1, /device:TPU:0, one launch (start us, length us, event | category | flops | bytes accessed | tf_op | source)
XLA Modules:
  0.0 313.9 jit_solution(4027525530323073326)
XLA Ops:
  15.8 1.9 constant_dynamic-slice_fusion.1
  21.4 45.0 %all-gather.12.cloned.1.call-done = f32[16,169,169]{2,1,0:T(8,128)} async-done(((f32[1,169,169]{2,1,0:T(8,128)}), f32[16,169,169]{2,1,0:T(8,128)}) %all-gather.12.cloned.1.call-update) | async-done | bytes 1827920 | tf_op jit(solution)/shard_map/all_gather | solution.py:18
  66.5 45.6 %all-gather.10.cloned.1.call-done = f32[16,169,169]{2,1,0:T(8,128)} async-done(((f32[1,169,169]{2,1,0:T(8,128)}), f32[16,169,169]{2,1,0:T(8,128)}) %all-gather.10.cloned.1.call-update) | async-done | bytes 1827920 | tf_op jit(solution)/shard_map/all_gather | solution.py:18
  112.0 81.1 %while.35 = (s32[]{:T(128)}, f32[1,169,169]{2,1,0:T(8,128)S(1)}, f32[1,169,169]{2,1,0:T(8,128)S(1)}, s32[]{:T(128)}, f32[16,1,169,169]{3,2,1,0:T(8,128)}, /*index=5*/f32[16,1,169,169]{3,2,1,0:T(8,128)}, s32[]{:T(128)}, s32[]{:T(128)}) while((s32[]{:T(128)}, f32[1,169,169]{2,1,0:T(8,128)S(1)}, f32[1,169,169]{2,1,0:T(8,128)S(1)}, ...), condition=%wide.region_1.2_spmd.clone, body=%wide.region_0.1_spmd.clone.sunk | while | flops 231886752 | bytes 2320444 | solution.py:31
  198.4 95.5 %while.36 = (s32[]{:T(128)}, f32[1,169,169]{1,2,0:T(8,128)S(1)}, f32[1,169,169]{1,2,0:T(8,128)S(1)}, s32[]{:T(128)}, f32[16,1,169,169]{3,2,1,0:T(8,128)}, /*inde...) while((s32[]{:T(128)}, f32[1,169,169]{1,2,0:T(8,128)S(1)}, ...), condition=%wide.region_3.4_spmd.clone, body=%wide.region_2.3_spmd.clone.sunk | while | flops 231886752 | bytes 2520487 | solution.py:31
  198.4 1.5 fusion.204
  199.9 1.5 fusion.202
  201.3 1.5 fusion.203
  202.8 1.5 fusion.205
  204.4 1.5 fusion.204
  207.3 1.5 fusion.203
  208.8 1.5 fusion.205
  210.3 1.5 fusion.204
  211.8 1.5 fusion.202
  213.3 1.5 fusion.203
  214.8 1.5 fusion.205
  216.3 1.5 fusion.204
  217.8 1.5 fusion.202
  219.2 1.5 fusion.203
  220.7 1.5 fusion.205
  222.3 1.5 fusion.204
  223.7 1.5 fusion.202
  225.2 1.5 fusion.203
  226.7 1.5 fusion.205
  228.2 1.5 fusion.204
  229.7 1.5 fusion.202
  231.2 1.5 fusion.203
  232.7 1.5 fusion.205
  234.2 1.5 fusion.204
  235.7 1.5 fusion.202
  237.1 1.5 fusion.203
  238.6 1.5 fusion.205
  240.2 1.5 fusion.204
  243.1 1.5 fusion.203
  244.6 1.5 fusion.205
  246.1 1.5 fusion.204
  247.6 1.5 fusion.202
  249.0 1.5 fusion.203
  250.6 1.5 fusion.205
  252.1 1.5 fusion.204
  255.0 1.5 fusion.203
  256.5 1.5 fusion.205
  258.1 1.5 fusion.204
  261.0 1.5 fusion.203
  262.5 1.5 fusion.205
  264.0 1.5 fusion.204
  265.5 1.5 fusion.202
  266.9 1.5 fusion.203
  268.4 1.5 fusion.205
  269.9 1.5 fusion.204
  271.4 1.5 fusion.202
  272.9 1.5 fusion.203
  274.4 1.5 fusion.205
  275.9 1.5 fusion.204
  277.4 1.5 fusion.202
  278.8 1.5 fusion.203
  280.3 1.5 fusion.205
  281.8 1.5 fusion.204
  284.8 1.5 fusion.203
  286.3 1.5 fusion.205
  287.8 1.5 fusion.204
  290.7 1.5 fusion.203
  292.2 1.5 fusion.205
  295.4 4.6 %reduce_sum.38 = f32[2,169,169]{2,0,1:T(2,128)S(1)} reduce(f32[16,1,2,169,169]{4,2,3,1,0:T(2,128)} %all-gather.8.cloned.1.call-done, f32[]{:T(128)} %constant.86.clone.1), dimensions={0,1}, to_apply=%region_4.5 | reduce | flops 856830 | bytes 3884300 | tf_op jit(solution)/shard_map/reduce_sum | solution.py:12
  (160 shorter events, 109.2 us)
Async XLA Ops:
  7.2 6.0 %copy-start = (f32[64,169]{1,0:T(8,128)S(1)}, f32[64,169]{1,0:T(8,128)}, u32[]{:S(2)}) copy-start(f32[64,169]{1,0:T(8,128)} %param.15) | copy-start | bytes 129796
  7.2 59.3 %all-gather.12.cloned.1.call-start = ((), (), s32[]{:S(2)}) async-start(), calls=%async_computation.2 | async-start | bytes 3063808 | tf_op jit(solution)/shard_map/all_gather | solution.py:18
  15.7 5.3 %copy-start.2 = (f32[16]{0:T(128)S(1)}, f32[16]{0:T(128)}, u32[]{:S(2)}) copy-start(f32[16]{0:T(128)} %param.19) | copy-start | bytes 196
  15.8 5.3 %copy-start.3 = (s32[16]{0:T(128)S(1)}, s32[16]{0:T(128)}, u32[]{:S(2)}) copy-start(s32[16]{0:T(128)} %param.18) | copy-start | bytes 196
  15.8 5.4 %copy-start.1 = (f32[1,2,169,169]{3,1,2,0:T(2,128)S(1)}, f32[1,2,169,169]{3,1,2,0:T(2,128)}, u32[]{:S(2)}) copy-start(f32[1,2,169,169]{3,1,2,0:T(2,128)} %param.17) | copy-start | bytes 685468
  19.2 92.8 %all-gather.10.cloned.1.call-start = ((), (), s32[]{:S(2)}) async-start(), calls=%async_computation.1 | async-start | bytes 3063808 | tf_op jit(solution)/shard_map/all_gather | solution.py:18
  20.8 274.6 %all-gather.8.cloned.1.call-start = ((), (), s32[]{:S(2)}) async-start(), calls=%async_computation | async-start | bytes 5883904 | tf_op jit(solution)/shard_map/all_gather | solution.py:11
Sparse Core Ops, SparseCore 0:
  19.4 47.0 all-gather.11
  69.3 42.6 all-gather.9
  198.5 55.9 all-gather.7
